TPU v7x, 32 devices: a whole 2x2x4 slice. The times are simulated.
32 devices in a mesh: groups: 2 (over y), feat: 4 (over z), pts: 2 (over x), sub: 2 (over core).
Axes of the slice: x: 2, y: 2, z: 4, core: 2. Of those that a mesh axis runs over, the one named last changes fastest.
Arguments:
- points: bfloat16 [256, 256], P(('groups', 'pts')), parts along dimension 0, may hold values from -6 to 6
- freqs: bfloat16 [256, 65536], P(None, ('feat', 'sub')), may hold values from -0.75 to 0.75
- phases: float32 [65536], P(('feat', 'sub')), may hold values from 0 to 6.283
- basis: bfloat16 [131072, 1024], P(('groups', 'feat', 'sub'), 'pts'), parts along dimension 0, may hold values from -0.0203125 to 0.0203125
Outputs:
- coefs: float32 [2048, 128], P('groups', 'pts'), parts along dimension 0
- new_basis: float32 [131072, 128], P(('groups', 'feat', 'sub'), 'pts'), parts along dimension 0
- factor: float32 [256, 128], P(('groups', 'pts')), parts along dimension 0
There are 2 independent parts, one for each index of `groups`. A program takes and returns all parts, laid end to end along the dimension named above; an argument that names none is the same for every part. Nothing has to cross between parts.
All inputs are finite; a program needn't handle non-finite values.
Results may differ from a plain program's by a relative error of at most 0.00055.
Values may be sent and summed in bfloat16 or wider, within the bound.
No kernel may reach another device: no remote copies, remote signals or barrier semaphores. Data moves between devices by JAX's collectives and lax.ppermute only.
A program may use at most 128 MiB of HBM per device.

v0:
```python
import jax
import jax.numpy as jnp
from jax import lax
from jax.sharding import PartitionSpec as P

FEATS = 65536


def on_device(points, freqs, phases, basis):
    highest = lax.Precision.HIGHEST
    phase_in = jnp.einsum("pd,df->fp", points, freqs, preferred_element_type=jnp.float32)
    features = jnp.cos(phase_in + phases[:, None])
    point_cols = features.shape[1]
    whole_basis = lax.all_gather(basis, "pts", axis=1, tiled=True).astype(jnp.float32)
    partial_value = jnp.einsum("fk,fp->kp", whole_basis, features, precision=highest)
    coefs = lax.psum(partial_value, ("feat", "sub"))
    fitted = jnp.dot(whole_basis, coefs, precision=highest)
    residual = features - fitted
    spread = lax.all_gather(residual, "pts", axis=1, tiled=True)
    block = jnp.einsum("fq,fp->qp", spread, residual, precision=highest)
    total_pts = block.shape[0]
    block = lax.psum(block, ("feat", "sub")) / FEATS
    gram = lax.all_gather(block, "pts", axis=1, tiled=True)
    factor = jnp.linalg.cholesky(gram)
    eye_mat = jnp.eye(total_pts, dtype=jnp.float32)
    inverse = jax.scipy.linalg.solve_triangular(factor, eye_mat, lower=True)
    offset = lax.axis_index("pts") * point_cols
    factor_rows = lax.dynamic_slice_in_dim(factor, offset, point_cols, 0)
    inv_rows = lax.dynamic_slice_in_dim(inverse, offset, point_cols, 0)
    new_basis = jnp.einsum("fq,pq->fp", spread, inv_rows, precision=highest)
    return (coefs, new_basis, factor_rows)


def solution(mesh):
    return jax.shard_map(
        on_device,
        mesh=mesh,
        in_specs=(
            P(("groups", "pts"), None),
            P(None, ("feat", "sub")),
            P(("feat", "sub")),
            P(("groups", "feat", "sub"), "pts"),
        ),
        out_specs=(
            P("groups", "pts"),
            P(("groups", "feat", "sub"), "pts"),
            P(("groups", "pts"), None),
        ),
        check_vma=False,
    )
```

profile of v0, /device:TPU:0, one launch (start us, length us, event | category | flops | bytes accessed | tf_op | source)
XLA Modules:
  0.0 432.8 jit_solution(4371246499104111773)
XLA Ops:
  7.2 0.0 copy-start
  7.2 0.0 copy-start.2
  7.2 0.0 all-gather.3.cloned.1.call-start
  7.2 0.7 all-gather.3.cloned.1.call-update
  7.9 0.0 all-reduce.2.cloned.1.call-start
  8.0 0.0 copy-done
  8.0 0.0 copy-done.2
  8.0 8.7 %fusion = f32[8192,64]{0,1:T(8,128)S(1)} fusion(bf16[64,256]{1,0:T(8,128)(2,1)S(1)} %copy-done, bf16[256,8192]{1,0:T(8,128)(2,1)} %param.5, f32[8192]{0:T(1024)S(1)} %copy-done.2), kind=kOutput, calls=%fused_computation.1 | convolution fusion | flops 268959744 | bytes 6356992 | tf_op jit(solution)/shard_map/pd,df->fp/dot_general | solution.py:11
  16.7 194.4 %all-gather.3.cloned.1.call-done = bf16[8192,1024]{1,0:T(8,128)(2,1)} async-done(((bf16[8192,512]{1,0:T(8,128)(2,1)}), bf16[8192,1024]{1,0:T(8,128)(2,1)}) %all-gather.3.cloned.1.call-update) | async-done | bytes 16777232 | tf_op jit(solution)/shard_map/all_gather | solution.py:14
  211.2 13.1 %convolution_bitcast_fusion.1 = f32[1024,64]{0,1:T(8,128)} fusion(f32[8192,64]{0,1:T(8,128)S(1)} %fusion, bf16[8192,1024]{1,0:T(8,128)(2,1)} %all-gather.3.cloned.1.call-done), kind=kOutput, calls=%fused_computation.4 | convolution fusion | flops 6442450944 | bytes 19136512 | tf_op jit(solution)/shard_map/fk,fp->kp/dot_general | solution.py:15
  224.3 0.0 all-reduce.2.cloned.1.call-update
  224.3 0.2 all-gather.5.cloned.1.call-start
  224.5 54.8 %all-reduce.2.cloned.1.call-done = f32[1024,64]{0,1:T(8,128)} async-done(((f32[1024,64]{0,1:T(8,128)}), f32[1024,64]{0,1:T(8,128)}) %all-reduce.2.cloned.1.call-update) | async-done | bytes 262160 | tf_op jit(solution)/shard_map/psum | solution.py:16
  279.4 19.7 %fusion.1 = f32[8192,64]{0,1:T(8,128)} fusion(f32[8192,64]{0,1:T(8,128)S(1)} %fusion, f32[1024,64]{0,1:T(8,128)} %all-reduce.2.cloned.1.call-done, bf16[8192,1024]{1,0:T(8,128)(2,1)} %all-gather.3.cloned.1.call-done), kind=kOutput, calls=%fused_computation.3 | convolution fusion | flops 6442975232 | bytes 21233664 | tf_op jit(solution)/shard_map/dot_general | solution.py:17
  299.1 0.0 all-gather.5.cloned.1.call-update
  299.1 55.9 %all-gather.5.cloned.1.call-done = f32[8192,128]{0,1:T(8,128)} async-done(((f32[8192,64]{0,1:T(8,128)}), f32[8192,128]{0,1:T(8,128)}) %all-gather.5.cloned.1.call-update) | async-done | bytes 4194320 | tf_op jit(solution)/shard_map/all_gather | solution.py:19
  355.0 7.3 %fusion.8 = f32[128,64]{0,1:T(8,128)S(1)} fusion(f32[8192,128]{0,1:T(8,128)} %all-gather.5.cloned.1.call-done, f32[8192,64]{0,1:T(8,128)} %fusion.1), kind=kOutput, calls=%fused_computation.20 | convolution fusion | flops 805306368 | bytes 6324224 | tf_op jit(solution)/shard_map/fq,fp->qp/dot_general | solution.py:20
  362.3 0.0 copy-start.1
  362.3 28.7 %psum.15 = f32[128,64]{0,1:T(8,128)S(1)} all-reduce(f32[128,64]{0,1:T(8,128)S(1)} %fusion.8), channel_id=1, replica_groups=mesh['groups'=2,'feat'=4,'pts'=2,'sub'=2] {'feat','sub'}, use_global_device_ids=true, to_apply=%region_1.0 | all-reduce | flops 8192 | bytes 65536 | tf_op jit(solution)/shard_map/psum | solution.py:22
  391.0 4.8 %all_gather.11 = f32[128,128]{0,1:T(8,128)S(1)} all-gather(f32[128,64]{0,1:T(8,128)S(1)} %broadcast_multiply_fusion), channel_id=1, replica_groups=mesh['groups'=2,'feat'=4,'pts'=2,'sub'=2] {'pts'}, dimensions={1}, use_global_device_ids=true | all-gather | bytes 98304 | tf_op jit(solution)/shard_map/all_gather | solution.py:23
  395.8 0.1 copy.7
  395.9 11.7 %cholesky.17 = f32[128,128]{1,0:T(8,128)S(1)} custom-call(f32[128,128]{1,0:T(8,128)S(1)} %fusion.4), custom_call_target="Cholesky" | custom-call | tf_op jit(solution)/shard_map/jit(cholesky)/cholesky | solution.py:24
  407.7 0.6 compare_reduce_fusion
  408.3 0.7 select_bitcast_fusion
  409.0 9.8 %custom-call.7 = f32[1,128,128]{1,2,0:T(8,128)S(1)} custom-call(f32[1,128,128]{2,1,0:T(8,128)S(1)} %get-tuple-element.3), custom_call_target="InvertDiagBlocksLowerTriangular" | custom-call | tf_op jit(solution)/shard_map/jit(_solve_triangular)/triangular_solve | solution.py:26
  418.8 0.2 fusion.2
  419.0 0.6 constant_dynamic-slice_fusion
  419.7 5.9 %fusion.5 = f32[8192,64]{0,1:T(8,128)} fusion(f32[8192,128]{0,1:T(8,128)} %all-gather.5.cloned.1.call-done, f32[128,128]{1,0:T(8,128)S(1)} %fusion.2, s32[]{:T(128)S(6)} %select_n.9), kind=kOutput, calls=%fused_computation.14 | convolution fusion | flops 805306368 | bytes 6324228 | tf_op jit(solution)/shard_map/fq,pq->fp/dot_general | solution.py:30
  425.6 0.0 copy-done.1
  425.6 0.7 copy.9
  (3 shorter events, 0.1 us)
Async XLA Ops:
  7.2 0.8 copy-start
  7.2 0.8 copy-start.2
  7.2 204.0 %all-gather.3.cloned.1.call-start = ((), (), s32[]{:S(2)}) async-start(), calls=%async_computation | async-start | bytes 25165824 | tf_op jit(solution)/shard_map/all_gather | solution.py:14
  7.9 271.5 %all-reduce.2.cloned.1.call-start = ((), (), s32[]{:S(2)}) async-start(), calls=%async_computation.1 | async-start | bytes 524288 | tf_op jit(solution)/shard_map/psum | solution.py:16
  224.3 130.7 %all-gather.5.cloned.1.call-start = ((), (), s32[]{:S(2)}) async-start(), calls=%async_computation.2 | async-start | bytes 6291456 | tf_op jit(solution)/shard_map/all_gather | solution.py:19
  362.3 63.3 %copy-start.1 = (f32[1024,64]{0,1:T(8,128)S(1)}, f32[1024,64]{0,1:T(8,128)}, u32[]{:S(2)}) copy-start(f32[1024,64]{0,1:T(8,128)} %all-reduce.2.cloned.1.call-done) | copy-start | bytes 786436
Sparse Core Ops, SparseCore 0:
  9.6 201.5 all-gather.2
  224.4 54.9 all-reduce.1
  299.3 55.7 all-gather.4
where the time goes:
time: 433 us
  waiting for transfers between devices  306 us (71%)
  matrix products  55 us (13%)
  blocking collectives  33.5 us (8%)
  other arithmetic  22.9 us (5%)
  between operations  13.8 us (3%)
    all_gather x1, waiting for transfers between devices, on_device(): lax.all_gather(basis, 'pts', axis=1, tiled=True).astype(jnp.float32)  194 us
    all_gather x1, waiting for transfers between devices, on_device(): spread = lax.all_gather(residual, 'pts', axis=1, tiled=True)  55.9 us
    psum x1, waiting for transfers between devices, on_device(): coefs = lax.psum(partial_value, ('feat', 'sub'))  54.8 us
    psum x1, blocking collectives, on_device(): block = lax.psum(block, ('feat', 'sub')) / FEATS  28.7 us
    dot_general x1, matrix products, on_device(): fitted = jnp.dot(whole_basis, coefs, precision=highest)  19.7 us
    dot_general x1, matrix products, on_device(): jnp.einsum('fk,fp->kp', whole_basis, features, precision=highest)  13.1 us
    another operation x3, other arithmetic, on_device(): factor = jnp.linalg.cholesky(gram)  12.4 us
    another operation x2, other arithmetic, on_device(): inverse = jax.scipy.linalg.solve_triangular(factor, eye_mat, lower=True)  10.5 us
  transfers between devices with their start and end apart: 3, of which 3 were waited for; matrix products, arithmetic and copies ran while one was open for 2% of the time, Pallas kernels for 0%

commit v1 on v0

--- a/solution.py
+++ b/solution.py
@@ -4,6 +4,12 @@
 from jax.sharding import PartitionSpec as P
 
 FEATS = 65536
+
+
+def add_all(x, name):
+    pieces = lax.all_gather(x, name, axis=0, tiled=False)
+    result = pieces.sum(axis=0)
+    return result
 
 
 def on_device(points, freqs, phases, basis):
@@ -19,7 +25,7 @@
     spread = lax.all_gather(residual, "pts", axis=1, tiled=True)
     block = jnp.einsum("fq,fp->qp", spread, residual, precision=highest)
     total_pts = block.shape[0]
-    block = lax.psum(block, ("feat", "sub")) / FEATS
+    block = add_all(block, ("feat", "sub")) / FEATS
     gram = lax.all_gather(block, "pts", axis=1, tiled=True)
     factor = jnp.linalg.cholesky(gram)
     eye_mat = jnp.eye(total_pts, dtype=jnp.float32)

time: 433 us -> 419 us (0.968)
  blocking collectives: 33.5 us -> 19.2 us
    psum x1 -> x0, blocking collectives: 28.7 us -> none  [on_device(): block = lax.psum(block, ('feat', 'sub')) / FEATS]
    all_gather x0 -> x1, blocking collectives: none -> 14.4 us  [add_all(): pieces = lax.all_gather(x, name, axis=0, tiled=False)]
where the time goes in v1:
time: 419 us
  waiting for transfers between devices  306 us (73%)
  matrix products  55 us (13%)
  other arithmetic  22.9 us (5%)
  blocking collectives  19.2 us (5%)
  between operations  13.8 us (3%)
    all_gather x1, waiting for transfers between devices, on_device(): lax.all_gather(basis, 'pts', axis=1, tiled=True).astype(jnp.float32)  194 us
    all_gather x1, waiting for transfers between devices, on_device(): spread = lax.all_gather(residual, 'pts', axis=1, tiled=True)  55.9 us
    psum x1, waiting for transfers between devices, on_device(): coefs = lax.psum(partial_value, ('feat', 'sub'))  54.8 us
    dot_general x1, matrix products, on_device(): fitted = jnp.dot(whole_basis, coefs, precision=highest)  19.7 us
    all_gather x1, blocking collectives, add_all(): pieces = lax.all_gather(x, name, axis=0, tiled=False)  14.4 us
    dot_general x1, matrix products, on_device(): jnp.einsum('fk,fp->kp', whole_basis, features, precision=highest)  13.1 us
    another operation x3, other arithmetic, on_device(): factor = jnp.linalg.cholesky(gram)  12.4 us
    another operation x2, other arithmetic, on_device(): inverse = jax.scipy.linalg.solve_triangular(factor, eye_mat, lower=True)  10.5 us
  transfers between devices with their start and end apart: 3, of which 3 were waited for; matrix products, arithmetic and copies ran while one was open for 2% of the time, Pallas kernels for 0%

profile of v1, /device:TPU:0, one launch (start us, length us, event | category | flops | bytes accessed | tf_op | source)
XLA Modules:
  0.0 418.7 jit_solution(9225830552464086406)
XLA Ops:
  7.2 0.0 copy-start
  7.2 0.0 copy-start.2
  7.2 0.0 all-gather.4.cloned.1.call-start
  7.2 0.7 all-gather.4.cloned.1.call-update
  7.9 0.0 all-reduce.2.cloned.1.call-start
  8.0 0.0 copy-done
  8.0 0.0 copy-done.2
  8.0 8.7 %fusion = f32[8192,64]{0,1:T(8,128)S(1)} fusion(bf16[64,256]{1,0:T(8,128)(2,1)S(1)} %copy-done, bf16[256,8192]{1,0:T(8,128)(2,1)} %param.5, f32[8192]{0:T(1024)S(1)} %copy-done.2), kind=kOutput, calls=%fused_computation.1 | convolution fusion | flops 268959744 | bytes 6356992 | tf_op jit(solution)/shard_map/pd,df->fp/dot_general | solution.py:17
  16.7 194.4 %all-gather.4.cloned.1.call-done = bf16[8192,1024]{1,0:T(8,128)(2,1)} async-done(((bf16[8192,512]{1,0:T(8,128)(2,1)}), bf16[8192,1024]{1,0:T(8,128)(2,1)}) %all-gather.4.cloned.1.call-update) | async-done | bytes 16777232 | tf_op jit(solution)/shard_map/all_gather | solution.py:20
  211.2 13.1 %convolution_bitcast_fusion.1 = f32[1024,64]{0,1:T(8,128)} fusion(f32[8192,64]{0,1:T(8,128)S(1)} %fusion, bf16[8192,1024]{1,0:T(8,128)(2,1)} %all-gather.4.cloned.1.call-done), kind=kOutput, calls=%fused_computation.4 | convolution fusion | flops 6442450944 | bytes 19136512 | tf_op jit(solution)/shard_map/fk,fp->kp/dot_general | solution.py:21
  224.3 0.0 all-reduce.2.cloned.1.call-update
  224.3 0.2 all-gather.6.cloned.1.call-start
  224.5 54.8 %all-reduce.2.cloned.1.call-done = f32[1024,64]{0,1:T(8,128)} async-done(((f32[1024,64]{0,1:T(8,128)}), f32[1024,64]{0,1:T(8,128)}) %all-reduce.2.cloned.1.call-update) | async-done | bytes 262160 | tf_op jit(solution)/shard_map/psum | solution.py:22
  279.4 19.7 %fusion.1 = f32[8192,64]{0,1:T(8,128)} fusion(f32[8192,64]{0,1:T(8,128)S(1)} %fusion, f32[1024,64]{0,1:T(8,128)} %all-reduce.2.cloned.1.call-done, bf16[8192,1024]{1,0:T(8,128)(2,1)} %all-gather.4.cloned.1.call-done), kind=kOutput, calls=%fused_computation.3 | convolution fusion | flops 6442975232 | bytes 21233664 | tf_op jit(solution)/shard_map/dot_general | solution.py:23
  299.1 0.0 all-gather.6.cloned.1.call-update
  299.1 55.9 %all-gather.6.cloned.1.call-done = f32[8192,128]{0,1:T(8,128)} async-done(((f32[8192,64]{0,1:T(8,128)}), f32[8192,128]{0,1:T(8,128)}) %all-gather.6.cloned.1.call-update) | async-done | bytes 4194320 | tf_op jit(solution)/shard_map/all_gather | solution.py:25
  355.0 7.3 %fusion.8 = f32[128,64]{0,1:T(8,128)S(1)} fusion(f32[8192,128]{0,1:T(8,128)} %all-gather.6.cloned.1.call-done, f32[8192,64]{0,1:T(8,128)} %fusion.1), kind=kOutput, calls=%fused_computation.21 | convolution fusion | flops 805306368 | bytes 6324224 | tf_op jit(solution)/shard_map/fq,fp->qp/dot_general | solution.py:26
  362.3 0.0 copy-start.1
  362.3 14.4 %all-gather = f32[1024,64]{0,1:T(8,128)S(1)} all-gather(f32[128,64]{0,1:T(8,128)S(1)} %fusion.8), channel_id=2, replica_groups=mesh['groups'=2,'feat'=4,'pts'=2,'sub'=2] {'feat','sub'}, dimensions={0}, use_global_device_ids=true | all-gather | bytes 294912 | tf_op jit(solution)/shard_map/all_gather | solution.py:10
  376.7 0.1 bitcast_reduce_fusion
  376.8 4.8 %all_gather.19 = f32[128,128]{0,1:T(8,128)S(1)} all-gather(f32[128,64]{0,1:T(8,128)S(1)} %broadcast_multiply_fusion), channel_id=1, replica_groups=mesh['groups'=2,'feat'=4,'pts'=2,'sub'=2] {'pts'}, dimensions={1}, use_global_device_ids=true | all-gather | bytes 98304 | tf_op jit(solution)/shard_map/all_gather | solution.py:29
  381.6 0.1 copy.7
  381.7 11.7 %cholesky.17 = f32[128,128]{1,0:T(8,128)S(1)} custom-call(f32[128,128]{1,0:T(8,128)S(1)} %fusion.4), custom_call_target="Cholesky" | custom-call | tf_op jit(solution)/shard_map/jit(cholesky)/cholesky | solution.py:30
  393.5 0.6 compare_reduce_fusion
  394.1 0.7 select_bitcast_fusion
  394.8 9.8 %custom-call.7 = f32[1,128,128]{1,2,0:T(8,128)S(1)} custom-call(f32[1,128,128]{2,1,0:T(8,128)S(1)} %get-tuple-element.3), custom_call_target="InvertDiagBlocksLowerTriangular" | custom-call | tf_op jit(solution)/shard_map/jit(_solve_triangular)/triangular_solve | solution.py:32
  404.6 0.2 fusion.2
  404.9 0.6 constant_dynamic-slice_fusion
  405.5 5.9 %fusion.5 = f32[8192,64]{0,1:T(8,128)} fusion(f32[8192,128]{0,1:T(8,128)} %all-gather.6.cloned.1.call-done, f32[128,128]{1,0:T(8,128)S(1)} %fusion.2, s32[]{:T(128)S(6)} %select_n.9), kind=kOutput, calls=%fused_computation.15 | convolution fusion | flops 805306368 | bytes 6324228 | tf_op jit(solution)/shard_map/fq,pq->fp/dot_general | solution.py:36
  411.4 0.0 copy-done.1
  411.4 0.7 copy.10
  (4 shorter events, 0.1 us)
Async XLA Ops:
  7.2 0.8 copy-start
  7.2 0.8 copy-start.2
  7.2 204.0 %all-gather.4.cloned.1.call-start = ((), (), s32[]{:S(2)}) async-start(), calls=%async_computation | async-start | bytes 25165824 | tf_op jit(solution)/shard_map/all_gather | solution.py:20
  7.9 271.5 %all-reduce.2.cloned.1.call-start = ((), (), s32[]{:S(2)}) async-start(), calls=%async_computation.1 | async-start | bytes 524288 | tf_op jit(solution)/shard_map/psum | solution.py:22
  224.3 130.7 %all-gather.6.cloned.1.call-start = ((), (), s32[]{:S(2)}) async-start(), calls=%async_computation.2 | async-start | bytes 6291456 | tf_op jit(solution)/shard_map/all_gather | solution.py:25
  362.3 49.1 %copy-start.1 = (f32[1024,64]{0,1:T(8,128)S(1)}, f32[1024,64]{0,1:T(8,128)}, u32[]{:S(2)}) copy-start(f32[1024,64]{0,1:T(8,128)} %all-reduce.2.cloned.1.call-done) | copy-start | bytes 786436
Sparse Core Ops, SparseCore 0:
  9.6 201.5 all-gather.3
  224.4 54.9 all-reduce.1
  299.3 55.7 all-gather.5
